TPU v7x, 32 devices: a whole 2x2x4 slice. The times are simulated.
32 devices in a mesh: batch: 4 (over y, x), filt: 8 (over z, core).
Axes of the slice: x: 2, y: 2, z: 4, core: 2. Of those that a mesh axis runs over, the one named last changes fastest.
Arguments:
- images: bfloat16 [768, 3072], P(('batch', 'filt')), may hold values from -6 to 6
- labels: int32 [768], P(('batch', 'filt')), may hold values from 0 to 9
- partner: int32 [768], P(('batch', 'filt')), may hold values from 0 to 767, as said below
- valid_mask: int32 [768], P(('batch', 'filt')), may hold values from 0 to 1, as said below
- group_sizes: int32 [4, 8], replicated, may hold values from 1 to 185, as said below
- stem_weight: float32 [16, 27], replicated, may hold values from -1.25 to 1.25
- bridge_weight: float32 [640, 16], P('filt'), may hold values from -1.5 to 1.5
- conv_weight: float32 [2, 640, 9, 640], P(None, 'filt'), may hold values from -0.078125 to 0.078125
- norm_params: float32 [6, 640], P(None, 'filt'), may hold values from 0.5 to 1.5
- head_weight: float32 [10, 640], P(None, 'filt'), may hold values from -1 to 1
- head_bias: float32 [10], replicated, may hold values from -3 to 3
- stem_first: float32 [16, 27], replicated, may hold values from -4.7683716e-06 to 4.7683716e-06
- stem_second: float32 [16, 27], replicated, may hold values from 1.2540817e-12 to 2.002716e-11
- bridge_first: float32 [640, 16], P('filt'), may hold values from -9.536743e-07 to 9.536743e-07
- bridge_second: float32 [640, 16], P('filt'), may hold values from 5.016327e-14 to 8.010864e-13
- conv_first: float32 [2, 640, 9, 640], P(None, 'filt'), may hold values from -2.3841858e-06 to 2.3841858e-06
- conv_second: float32 [2, 640, 9, 640], P(None, 'filt'), may hold values from 3.5671658e-13 to 5.6966146e-12
- norm_first: float32 [6, 640], P(None, 'filt'), may hold values from -7.6293945e-06 to 7.6293945e-06
- norm_second: float32 [6, 640], P(None, 'filt'), may hold values from 3.2104493e-12 to 5.126953e-11
- head_first: float32 [10, 640], P(None, 'filt'), may hold values from -7.6293945e-06 to 7.6293945e-06
- head_second: float32 [10, 640], P(None, 'filt'), may hold values from 3.2104493e-12 to 5.126953e-11
- bias_first: float32 [10], replicated, may hold values from -2.2888184e-05 to 2.2888184e-05
- bias_second: float32 [10], replicated, may hold values from 3.5671657e-11 to 5.696615e-10
Outputs:
- stem_weight_new: float32 [16, 27], replicated
- stem_first_new: float32 [16, 27], replicated
- stem_second_new: float32 [16, 27], replicated
- bridge_weight_new: float32 [640, 16], P('filt')
- bridge_first_new: float32 [640, 16], P('filt')
- bridge_second_new: float32 [640, 16], P('filt')
- conv_weight_new: float32 [2, 640, 9, 640], P(None, 'filt')
- conv_first_new: float32 [2, 640, 9, 640], P(None, 'filt')
- conv_second_new: float32 [2, 640, 9, 640], P(None, 'filt')
- norm_params_new: float32 [6, 640], P(None, 'filt')
- norm_first_new: float32 [6, 640], P(None, 'filt')
- norm_second_new: float32 [6, 640], P(None, 'filt')
- head_weight_new: float32 [10, 640], P(None, 'filt')
- head_first_new: float32 [10, 640], P(None, 'filt')
- head_second_new: float32 [10, 640], P(None, 'filt')
- head_bias_new: float32 [10], replicated
- bias_first_new: float32 [10], replicated
- bias_second_new: float32 [10], replicated
- grad_norm: float32 [], replicated
- loss: float32 [], replicated
Inputs may be any that keep to these rules, and one draw needn't show every extreme that they name: `group_sizes`: row b lists the sizes of the 8 groups of batch shard b, laid one after another from the shard's first slot; a shard's sizes sum to at most 192, and in one shard exactly. `valid_mask`: slots after a shard's groups hold 0; the first slot of every group holds 1, and so does image 768 - 1. `partner`: each entry is the index of an image whose valid_mask is 1.
All inputs are finite; a program needn't handle non-finite values.
Results may differ from a plain program's by a relative error of at most 0.008.
The roundings to bfloat16 on the way count: a program that leaves them out, or rounds other values in their place, can miss the bound.
Values may be sent and summed in bfloat16 or wider, within the bound.
A program may use at most 256 MiB of HBM per device.

v0:
```python
import jax
import jax.numpy as jnp
from jax import lax
from jax.sharding import PartitionSpec as P

STEP = 8
beta_one = 0.9
beta_two = 0.95
adam_eps = 1e-08
norm_epsilon = 1e-05
clip_norm = 0.01
own_share = 0.7


def make_patches(images):
    number = images.shape[0]
    grid = images.reshape(number, 3, 32, 32)
    padded = jnp.pad(grid, ((0, 0), (0, 0), (1, 1), (1, 1)))
    pieces = [
        padded[:, :, row_off : row_off + 29 : 4, col_off : col_off + 29 : 4]
        for row_off in range(3)
        for col_off in range(3)
    ]
    stacked = jnp.stack(pieces, axis=2)
    return jnp.transpose(stacked, (1, 2, 0, 3, 4)).reshape(27, number * 64)


def shifted(feature_field):
    width, rows = feature_field.shape
    grid = feature_field.reshape(width, rows // 64, 8, 8)
    padded = jnp.pad(grid, ((0, 0), (0, 0), (1, 1), (1, 1)))
    pieces = [
        padded[:, :, row_off : row_off + 8, col_off : col_off + 8]
        for row_off in range(3)
        for col_off in range(3)
    ]
    return jnp.stack(pieces, axis=0).reshape(9 * width, rows)


def unshifted(parts, width):
    rows = parts.shape[1]
    grid = parts.reshape(9, width, rows // 64, 8, 8)
    summed = jnp.zeros((width, rows // 64, 10, 10), jnp.float32)
    for row_off in range(3):
        for col_off in range(3):
            summed = summed + jnp.pad(
                grid[3 * row_off + col_off],
                ((0, 0), (0, 0), (row_off, 2 - row_off), (col_off, 2 - col_off)),
            )
    return summed[:, :, 1:9, 1:9].reshape(width, rows)


def image_weights(valid_mask, group_sizes):
    shards, groups = group_sizes.shape
    capacity = valid_mask.shape[0] // shards
    group_ends = jnp.cumsum(group_sizes, axis=1)
    slot_index = jnp.arange(capacity, dtype=jnp.int32)
    member = jnp.sum(
        (slot_index[None, :, None] >= group_ends[:, None, :]).astype(jnp.int32), axis=2
    )
    member = jnp.minimum(member, groups - 1)
    chosen = (member[:, :, None] == jnp.arange(groups, dtype=jnp.int32)[None, None, :]).astype(
        jnp.float32
    )
    sizes_each = jnp.sum(chosen * group_sizes[:, None, :].astype(jnp.float32), axis=2)
    return valid_mask.astype(jnp.float32) / sizes_each.reshape(-1)


def norm_forward(feature_field, norm_gain, norm_shift, row_validity_mask, valid_count):
    batch_mean = (
        lax.psum(jnp.sum(feature_field * row_validity_mask, axis=1), ("batch", "filt"))
        / valid_count
    )
    centered_input = feature_field - batch_mean[:, None]
    batch_variance = (
        lax.psum(
            jnp.sum(centered_input * centered_input * row_validity_mask, axis=1), ("batch", "filt")
        )
        / valid_count
    )
    inverse_scale = lax.rsqrt(batch_variance + norm_epsilon)
    normalized_input = (feature_field - batch_mean[:, None]) * inverse_scale[:, None]
    norm_output = jnp.maximum(norm_gain[:, None] * normalized_input + norm_shift[:, None], 0.0)
    return (norm_output, normalized_input, inverse_scale)


def masked_norm_backward(
    output_gradient,
    norm_output,
    normalized_input,
    inverse_scale,
    norm_gain,
    row_validity_mask,
    valid_count,
):
    passed_rows = jnp.where(norm_output > 0.0, output_gradient, 0.0)
    shift_gradient, gain_gradient = lax.psum(
        (jnp.sum(passed_rows, axis=1), jnp.sum(passed_rows * normalized_input, axis=1)),
        ("batch", "filt"),
    )
    input_gradient = (
        passed_rows
        - row_validity_mask[None, :]
        * (shift_gradient[:, None] + normalized_input * gain_gradient[:, None])
        / valid_count
    )
    return ((norm_gain * inverse_scale)[:, None] * input_gradient, gain_gradient, shift_gradient)


def conv_forward(feature_field, weight_shard):
    stacked = shifted(feature_field)
    low_shard = weight_shard.astype(jnp.bfloat16)
    piece = lax.all_gather(low_shard, "filt", axis=0, tiled=True)
    norm_output = jnp.dot(
        piece.reshape(piece.shape[0], -1), stacked, preferred_element_type=jnp.float32
    )
    return (norm_output, None)


def conv_backward(feature_field, weight_shard, output_gradient):
    width = feature_field.shape[0]
    stacked = shifted(feature_field)
    rows_grad = output_gradient
    term = lax.dot_general(
        rows_grad, stacked, (((1,), (1,)), ((), ())), preferred_element_type=jnp.float32
    )
    weight_grad = lax.psum_scatter(
        term.reshape(lax.axis_size("filt") * weight_shard.shape[0], 9, width),
        "filt",
        scatter_dimension=0,
        tiled=True,
    )
    piece = lax.all_gather(weight_shard.astype(jnp.bfloat16), "filt", axis=0, tiled=True)
    rows_grad = output_gradient
    back = lax.dot_general(
        piece.reshape(piece.shape[0], -1),
        rows_grad,
        (((0,), (0,)), ((), ())),
        preferred_element_type=jnp.float32,
    )
    return (unshifted(back, width), weight_grad)


def adam_step(weight, output_gradient, first, second, rate, shrink, factor):
    clipped = output_gradient * factor
    first = beta_one * first + (1.0 - beta_one) * clipped
    second = beta_two * second + (1.0 - beta_two) * clipped * clipped
    ahead = first / (1.0 - beta_one**STEP)
    behind = second / (1.0 - beta_two**STEP)
    return (
        weight - rate * (ahead / (jnp.sqrt(behind) + adam_eps) + shrink * weight),
        first,
        second,
    )


def body(
    images,
    labels,
    partner,
    valid_mask,
    group_sizes,
    stem_weight,
    bridge_weight,
    conv_weight,
    norm_params,
    head_weight,
    head_bias,
    stem_first,
    stem_second,
    bridge_first,
    bridge_second,
    conv_first,
    conv_second,
    norm_first,
    norm_second,
    head_first,
    head_second,
    bias_first,
    bias_second,
):
    width = bridge_weight.shape[0]
    bridge_all, norm_all, head_all = (
        lax.all_gather(bridge_weight, "filt", axis=0, tiled=True),
        lax.all_gather(norm_params, "filt", axis=1, tiled=True),
        lax.all_gather(head_weight, "filt", axis=1, tiled=True),
    )
    labels_all, valid_all = (
        lax.all_gather(labels, ("batch", "filt"), axis=0, tiled=True),
        lax.all_gather(valid_mask, ("batch", "filt"), axis=0, tiled=True),
    )
    weight_all = image_weights(valid_all, group_sizes)
    total = jnp.sum(weight_all)
    valid_count = 64.0 * jnp.sum(valid_all.astype(jnp.float32))
    local = images.shape[0]
    image_weight = lax.dynamic_slice_in_dim(
        weight_all, lax.axis_index(("batch", "filt")) * local, local
    )
    row_validity_mask = jnp.repeat(valid_mask.astype(jnp.float32), 64)
    patch = make_patches(images)
    stem = jnp.dot(
        stem_weight.astype(jnp.bfloat16), patch, preferred_element_type=jnp.float32
    ).astype(jnp.bfloat16)
    base = jnp.dot(bridge_all.astype(jnp.bfloat16), stem, preferred_element_type=jnp.float32)
    first, first_hat, first_scale = norm_forward(
        base, norm_all[0], norm_all[1], row_validity_mask, valid_count
    )
    first_low = first.astype(jnp.bfloat16)
    inner, kept_zero = conv_forward(first_low, conv_weight[0])
    second, second_hat, second_scale = norm_forward(
        inner, norm_all[2], norm_all[3], row_validity_mask, valid_count
    )
    second_low = second.astype(jnp.bfloat16)
    branch, kept_one = conv_forward(second_low, conv_weight[1])
    final, final_hat, final_scale = norm_forward(
        base + branch, norm_all[4], norm_all[5], row_validity_mask, valid_count
    )
    pooled = jnp.mean(final.reshape(final.shape[0], local, 64), axis=2).astype(jnp.bfloat16)
    logits = (
        jnp.dot(head_all.astype(jnp.bfloat16), pooled, preferred_element_type=jnp.float32)
        + head_bias[:, None]
    )
    moved = logits - jnp.max(logits, axis=0, keepdims=True)
    logp = moved - jnp.log(jnp.sum(jnp.exp(moved), axis=0, keepdims=True))
    classes = jnp.arange(logits.shape[0], dtype=jnp.int32)
    partner_labels = jnp.take(labels_all, partner)
    target = own_share * (labels[None, :] == classes[:, None]).astype(jnp.float32) + (
        1.0 - own_share
    ) * (partner_labels[None, :] == classes[:, None]).astype(jnp.float32)
    loss_part = -jnp.sum(image_weight * jnp.sum(target * logp, axis=0))
    d_logits = ((jnp.exp(logp) - target) * (image_weight / total)[None, :]).astype(jnp.bfloat16)
    bias_grad = jnp.sum(d_logits.astype(jnp.float32), axis=1)
    head_grad = lax.dot_general(
        d_logits, pooled, (((1,), (1,)), ((), ())), preferred_element_type=jnp.float32
    )
    d_pooled = lax.dot_general(
        head_all.astype(jnp.bfloat16),
        d_logits,
        (((0,), (0,)), ((), ())),
        preferred_element_type=jnp.float32,
    )
    d_final = jnp.repeat(d_pooled / 64.0, 64, axis=1)
    d_block, gain_two, shift_two = masked_norm_backward(
        d_final, final, final_hat, final_scale, norm_all[4], row_validity_mask, valid_count
    )
    d_second, conv_grad_one = conv_backward(
        second_low, conv_weight[1], d_block.astype(jnp.bfloat16)
    )
    d_inner, gain_one, shift_one = masked_norm_backward(
        d_second, second, second_hat, second_scale, norm_all[2], row_validity_mask, valid_count
    )
    d_first, conv_grad_zero = conv_backward(first_low, conv_weight[0], d_inner.astype(jnp.bfloat16))
    d_lower, gain_zero, shift_zero = masked_norm_backward(
        d_first, first, first_hat, first_scale, norm_all[0], row_validity_mask, valid_count
    )
    d_base = (d_block + d_lower).astype(jnp.bfloat16)
    bridge_grad = lax.dot_general(
        d_base, stem, (((1,), (1,)), ((), ())), preferred_element_type=jnp.float32
    )
    d_stem = lax.dot_general(
        bridge_all.astype(jnp.bfloat16),
        d_base,
        (((0,), (0,)), ((), ())),
        preferred_element_type=jnp.float32,
    ).astype(jnp.bfloat16)
    stem_grad = lax.dot_general(
        d_stem, patch, (((1,), (1,)), ((), ())), preferred_element_type=jnp.float32
    )
    bridge_part, head_part = (
        lax.psum_scatter(bridge_grad, "filt", scatter_dimension=0, tiled=True),
        lax.psum_scatter(head_grad, "filt", scatter_dimension=1, tiled=True),
    )
    conv_grad, bridge_sum, head_sum = lax.psum(
        (jnp.stack([conv_grad_zero, conv_grad_one]), bridge_part, head_part), "batch"
    )
    stem_sum, bias_sum, loss_sum = lax.psum((stem_grad, bias_grad, loss_part), ("batch", "filt"))
    norm_full = jnp.stack([gain_zero, shift_zero, gain_one, shift_one, gain_two, shift_two])
    norm_grad = lax.dynamic_slice_in_dim(norm_full, lax.axis_index("filt") * width, width, 1)
    owned_square = (
        jnp.sum(conv_grad * conv_grad)
        + jnp.sum(bridge_sum * bridge_sum)
        + jnp.sum(norm_grad * norm_grad)
        + jnp.sum(head_sum * head_sum)
    )
    squares_all = (
        lax.psum(owned_square, "filt") + jnp.sum(stem_sum * stem_sum) + jnp.sum(bias_sum * bias_sum)
    )
    grad_norm = jnp.sqrt(squares_all)
    factor = clip_norm / jnp.maximum(grad_norm, clip_norm)
    stem_new = adam_step(stem_weight, stem_sum, stem_first, stem_second, 0.5, 0.05, factor)
    bridge_new = adam_step(
        bridge_weight, bridge_sum, bridge_first, bridge_second, 0.6, 0.05, factor
    )
    conv_new = adam_step(conv_weight, conv_grad, conv_first, conv_second, 0.033, 0.05, factor)
    norm_new = adam_step(norm_params, norm_grad, norm_first, norm_second, 0.5, 0.0, factor)
    head_new = adam_step(head_weight, head_sum, head_first, head_second, 0.1, 0.05, factor)
    bias_new = adam_step(head_bias, bias_sum, bias_first, bias_second, 0.5, 0.0, factor)
    return (
        stem_new[0],
        stem_new[1],
        stem_new[2],
        bridge_new[0],
        bridge_new[1],
        bridge_new[2],
        conv_new[0],
        conv_new[1],
        conv_new[2],
        norm_new[0],
        norm_new[1],
        norm_new[2],
        head_new[0],
        head_new[1],
        head_new[2],
        bias_new[0],
        bias_new[1],
        bias_new[2],
        grad_norm,
        loss_sum / total,
    )


def solution(mesh):
    in_specs = (
        P(("batch", "filt"), None),
        P(("batch", "filt")),
        P(("batch", "filt")),
        P(("batch", "filt")),
        P(),
        P(),
        P("filt", None),
        P(None, "filt", None, None),
        P(None, "filt"),
        P(None, "filt"),
        P(),
        P(),
        P(),
        P("filt", None),
        P("filt", None),
        P(None, "filt", None, None),
        P(None, "filt", None, None),
        P(None, "filt"),
        P(None, "filt"),
        P(None, "filt"),
        P(None, "filt"),
        P(),
        P(),
    )
    out_specs = (
        P(),
        P(),
        P(),
        P("filt", None),
        P("filt", None),
        P("filt", None),
        P(None, "filt", None, None),
        P(None, "filt", None, None),
        P(None, "filt", None, None),
        P(None, "filt"),
        P(None, "filt"),
        P(None, "filt"),
        P(None, "filt"),
        P(None, "filt"),
        P(None, "filt"),
        P(),
        P(),
        P(),
        P(),
        P(),
    )
    return jax.shard_map(body, mesh=mesh, in_specs=in_specs, out_specs=out_specs, check_vma=False)
```

profile of v0, /device:TPU:0, one launch (start us, length us, event | category | flops | bytes accessed | tf_op | source)
XLA Modules:
  0.0 1185.0 jit_solution(9924384892840319865)
XLA Ops:
  22.0 15.9 %all-gather.3 = bf16[8,80,16]{1,2,0:T(8,128)(2,1)S(1)} all-gather(bf16[1,80,16]{1,2,0:T(8,128)(2,1)S(1)} %bitcast_convert_fusion.1), channel_id=1, replica_groups=mesh['batch'=4,'filt'=8] {'filt'}, dimensions={0}, use_global_device_ids=true | all-gather | bytes 23040 | tf_op jit(solution)/shard_map/all_gather | solution.py:184
  38.4 14.2 %all-gather.2 = f32[8,80,6]{1,2,0:T(8,128)S(1)} all-gather(f32[1,80,6]{1,2,0:T(8,128)S(1)} %bitcast.381), channel_id=1, replica_groups=mesh['batch'=4,'filt'=8] {'filt'}, dimensions={0}, use_global_device_ids=true | all-gather | bytes 17280 | tf_op jit(solution)/shard_map/all_gather | solution.py:185
  53.4 42.8 %all-reduce.23 = (s32[768]{0:T(1024)S(1)}, s32[768]{0:T(1024)S(1)}) all-reduce(s32[768]{0:T(1024)S(1)} %dynamic-update-slice, s32[768]{0:T(1024)S(1)} %dynamic-update-slice.1), channel_id=1, replica_groups=mesh['batch'=4,'filt'=8] {'batch','filt'}, use_global_device_ids=true, to_apply=%add.21 | all-reduce | flops 1536 | bytes 12288
  100.1 43.6 %psum.133 = f32[640]{0:T(1024)S(1)} all-reduce(f32[640]{0:T(1024)S(1)} %get-tuple-element.111), channel_id=1, replica_groups=mesh['batch'=4,'filt'=8] {'batch','filt'}, use_global_device_ids=true, to_apply=%region_1.2 | all-reduce | flops 640 | bytes 5120 | tf_op jit(solution)/shard_map/psum | solution.py:71
  146.4 41.4 %psum.134 = f32[640]{0:T(1024)S(1)} all-reduce(f32[640]{0:T(1024)S(1)} %multiply_reduce_fusion.4), channel_id=1, replica_groups=mesh['batch'=4,'filt'=8] {'batch','filt'}, use_global_device_ids=true, to_apply=%region_4.5 | all-reduce | flops 640 | bytes 5120 | tf_op jit(solution)/shard_map/psum | solution.py:76
  203.1 14.7 %all-gather.4 = bf16[8,80,10]{1,2,0:T(8,128)(2,1)S(1)} all-gather(bf16[1,80,10]{1,2,0:T(8,128)(2,1)S(1)} %bitcast_convert_fusion), channel_id=1, replica_groups=mesh['batch'=4,'filt'=8] {'filt'}, dimensions={0}, use_global_device_ids=true | all-gather | bytes 14400 | tf_op jit(solution)/shard_map/all_gather | solution.py:186
  236.9 12.4 %copy.154 = bf16[1,640,9,640]{1,3,2,0:T(8,128)(2,1)} copy(bf16[1,640,9,640]{3,1,2,0:T(8,128)(2,1)} %all-gather.8.cloned.1.call-done) | data formatting | bytes 14745600 | tf_op jit(solution)/shard_map/all_gather | solution.py:113
  249.3 20.4 %multiply_reduce_fusion.3 = (f32[640]{0:T(1024)S(1)}, f32[1536,640]{1,0:T(8,128)}) fusion(f32[1536]{0:T(1024)S(1)} %mul.497, bf16[5760,1536]{0,1:T(8,128)(2,1)} %bitcast.334, bf16[640,5760]{0,1:T(8,128)(2,1)} %bitcast.371), kind=kOutput, calls=%fused_computation.73 | convolution fusion | flops 11326585856 | bytes 29008384 | tf_op jit(solution)/shard_map/dot_general | solution.py:114
  269.7 38.4 %psum.135 = f32[640]{0:T(1024)S(1)} all-reduce(f32[640]{0:T(1024)S(1)} %get-tuple-element.113), channel_id=1, replica_groups=mesh['batch'=4,'filt'=8] {'batch','filt'}, use_global_device_ids=true, to_apply=%region_6.7 | all-reduce | flops 640 | bytes 5120 | tf_op jit(solution)/shard_map/psum | solution.py:71
  310.8 41.8 %psum.136 = f32[640]{0:T(1024)S(1)} all-reduce(f32[640]{0:T(1024)S(1)} %multiply_reduce_fusion.2), channel_id=1, replica_groups=mesh['batch'=4,'filt'=8] {'batch','filt'}, use_global_device_ids=true, to_apply=%region_8.9 | all-reduce | flops 640 | bytes 5120 | tf_op jit(solution)/shard_map/psum | solution.py:76
  367.0 12.4 %copy.156 = bf16[1,640,9,640]{1,3,2,0:T(8,128)(2,1)} copy(bf16[1,640,9,640]{3,1,2,0:T(8,128)(2,1)} %all-gather.10.cloned.1.call-done) | data formatting | bytes 14745600 | tf_op jit(solution)/shard_map/all_gather | solution.py:113
  379.4 20.7 %multiply_reduce_fusion.1 = (f32[640]{0:T(1024)S(1)}, f32[1536,640]{1,0:T(8,128)}) fusion(f32[1536]{0:T(1024)S(1)} %mul.497, f32[1536,640]{1,0:T(8,128)} %get-tuple-element.112, bf16[5760,1536]{0,1:T(8,128)(2,1)} %bitcast.335, bf16[640,5760]{0,1:T(8,128)(2,1)} %bitcast.373), kind=kOutput, calls=%fused_computation.70 | convolution fusion | flops 11327568896 | bytes 32940544 | tf_op jit(solution)/shard_map/dot_general | solution.py:114
  400.1 38.6 %psum.137 = f32[640]{0:T(1024)S(1)} all-reduce(f32[640]{0:T(1024)S(1)} %get-tuple-element.115), channel_id=1, replica_groups=mesh['batch'=4,'filt'=8] {'batch','filt'}, use_global_device_ids=true, to_apply=%region_10.11 | all-reduce | flops 640 | bytes 5120 | tf_op jit(solution)/shard_map/psum | solution.py:71
  441.4 41.9 %psum.138 = f32[640]{0:T(1024)S(1)} all-reduce(f32[640]{0:T(1024)S(1)} %multiply_reduce_fusion), channel_id=1, replica_groups=mesh['batch'=4,'filt'=8] {'batch','filt'}, use_global_device_ids=true, to_apply=%region_12.13 | all-reduce | flops 640 | bytes 5120 | tf_op jit(solution)/shard_map/psum | solution.py:76
  495.4 38.8 %all-reduce.27 = (f32[640]{0:T(1024)S(1)}, f32[640]{0:T(1024)S(1)}) all-reduce(f32[640]{0:T(1024)S(1)} %get-tuple-element.25, f32[640]{0:T(1024)S(1)} %get-tuple-element.24), channel_id=1, replica_groups=mesh['batch'=4,'filt'=8] {'batch','filt'}, use_global_device_ids=true, to_apply=%region_23.24 | all-reduce | flops 1280 | bytes 10240 | tf_op jit(solution)/shard_map/psum | solution.py:97
  539.9 24.1 %convolution_bitcast_fusion.1 = f32[5760,1536]{0,1:T(8,128)} fusion(bf16[640,5760]{0,1:T(8,128)(2,1)} %bitcast.374, f32[640,1536]{0,1:T(8,128)} %fusion.4), kind=kOutput, calls=%fused_computation.2 | convolution fusion | flops 11325603840 | bytes 46694400 | tf_op jit(solution)/shard_map/dot_general | solution.py:135
  564.0 22.5 %fusion.63 = (f32[640,1536]{0,1:T(8,128)}, f32[640,1536]{0,1:T(8,128)S(1)}, f32[640,1536]{0,1:T(8,128)}, f32[640,1536]{0,1:T(8,128)}, f32[640,1536]{0,1:T(8,128)...) fusion(f32[5760,1536]{0,1:T(8,128)} %convolution_bitcast_fusion.1), kind=kLoop, calls=%fused_computation.220 | loop fusion | bytes 70778880 | tf_op jit(solution)/shard_map/slice | solution.py:47
  586.6 10.3 pad_add_fusion.1
  596.9 10.2 pad_add_fusion.8
  609.1 41.4 %all-reduce.26 = (f32[640]{0:T(1024)S(1)}, f32[640]{0:T(1024)S(1)}) all-reduce(f32[640]{0:T(1024)S(1)} %get-tuple-element.23, f32[640]{0:T(1024)S(1)} %get-tuple-element.22), channel_id=1, replica_groups=mesh['batch'=4,'filt'=8] {'batch','filt'}, use_global_device_ids=true, to_apply=%region_27.28 | all-reduce | flops 1280 | bytes 10240 | tf_op jit(solution)/shard_map/psum | solution.py:97
  656.0 18.0 %fusion.31 = f32[640,9,640]{2,0,1:T(8,128)} fusion(bf16[9,640,1536]{1,2,0:T(8,128)(2,1)} %constant_dynamic-update-slice_fusion.11, bf16[640,1536]{0,1:T(8,128)(2,1)S(1)} %fusion.24), kind=kOutput, calls=%fused_computation.96 | convolution fusion | flops 11324620800 | bytes 34406400 | tf_op jit(solution)/shard_map/dot_general | solution.py:124
  692.6 18.0 %fusion.29 = f32[640,9,640]{2,0,1:T(8,128)} fusion(bf16[9,640,1536]{1,2,0:T(8,128)(2,1)} %constant_dynamic-update-slice_fusion.19, f32[640,1536]{0,1:T(8,128)S(1)} %copy-done.6), kind=kOutput, calls=%fused_computation.93 | convolution fusion | flops 11325603840 | bytes 36372480 | tf_op jit(solution)/shard_map/dot_general | solution.py:124
  712.1 21.5 %convolution_bitcast_fusion = f32[5760,1536]{0,1:T(8,128)} fusion(bf16[640,1536]{0,1:T(8,128)(2,1)S(1)} %copy-done.8, bf16[640,5760]{0,1:T(8,128)(2,1)} %bitcast.372), kind=kOutput, calls=%fused_computation.1 | convolution fusion | flops 11324620800 | bytes 44728320 | tf_op jit(solution)/shard_map/dot_general | solution.py:135
  733.6 24.1 %fusion.62 = (f32[640,1536]{0,1:T(8,128)}, f32[640,1536]{0,1:T(8,128)}, f32[640,1536]{0,1:T(8,128)}, f32[640,1536]{0,1:T(8,128)}, f32[640,1536]{0,1:T(8,128)}, /...) fusion(f32[5760,1536]{0,1:T(8,128)} %convolution_bitcast_fusion), kind=kLoop, calls=%fused_computation.219 | loop fusion | bytes 70778880 | tf_op jit(solution)/shard_map/slice | solution.py:47
  775.5 40.8 %all-reduce.25 = (f32[640]{0:T(1024)S(1)}, f32[640]{0:T(1024)S(1)}) all-reduce(f32[640]{0:T(1024)S(1)} %get-tuple-element.21, f32[640]{0:T(1024)S(1)} %get-tuple-element.20), channel_id=1, replica_groups=mesh['batch'=4,'filt'=8] {'batch','filt'}, use_global_device_ids=true, to_apply=%region_31.32 | all-reduce | flops 1280 | bytes 10240 | tf_op jit(solution)/shard_map/psum | solution.py:97
  825.0 149.3 %reduce-scatter.11.cloned.1.call-done = f32[80,9,640]{2,0,1:T(8,128)} async-done(((f32[640,9,640]{2,0,1:T(8,128)}), f32[80,9,640]{2,0,1:T(8,128)}) %reduce-scatter.11.cloned.1.call-update) | async-done | bytes 1843216 | tf_op jit(solution)/shard_map/reduce_scatter | solution.py:127
  982.4 38.0 %all-reduce.24 = (f32[16,27]{1,0:T(8,128)S(1)}, f32[10]{0:T(128)S(1)}, f32[]{:T(128)}) all-reduce(f32[16,27]{1,0:T(8,128)S(1)} %fusion.36, f32[10]{0:T(128)S(1)} %copy-done.53, f32[]{:T(128)S(6)} %neg.3), channel_id=1, replica_groups=mesh['batch'=4,'filt'=8] {'batch','filt'}, use_global_device_ids=true, to_apply=%region_32.33 | all-reduce | flops 443 | bytes 3544 | tf_op jit(solution)/shard_map/psum | solution.py:276
  1022.4 15.1 %reduce-scatter.13.cloned.1.call-done = f32[80,16]{1,0:T(8,128)} async-done(((f32[640,16]{1,0:T(8,128)}), f32[80,16]{1,0:T(8,128)}) %reduce-scatter.13.cloned.1.call-update) | async-done | bytes 5136
  1038.4 16.5 %all-reduce.28 = (f32[80,16]{0,1:T(8,128)S(1)}, f32[10,80]{1,0:T(8,128)S(1)}) all-reduce(f32[80,16]{0,1:T(8,128)S(1)} %copy.169, f32[10,80]{1,0:T(8,128)S(1)} %copy.171), channel_id=1, replica_groups=mesh['batch'=4,'filt'=8] {'batch'}, use_global_device_ids=true, to_apply=%region_38.39 | all-reduce | flops 2080 | bytes 16640 | tf_op jit(solution)/shard_map/psum | solution.py:273
  1056.1 79.8 %all-reduce.31.cloned.1.call-done = f32[2,80,9,640]{3,1,2,0:T(8,128)} async-done(((f32[2,80,9,640]{3,1,2,0:T(8,128)}), f32[2,80,9,640]{3,1,2,0:T(8,128)}) %all-reduce.31.cloned.1.call-update) | async-done | bytes 3686416 | tf_op jit(solution)/shard_map/psum | solution.py:273
  1143.4 16.9 %psum.149 = f32[]{:T(128)} all-reduce(f32[]{:T(128)S(6)} %add.378), channel_id=1, replica_groups=mesh['batch'=4,'filt'=8] {'filt'}, use_global_device_ids=true, to_apply=%region_44.45 | all-reduce | flops 1 | bytes 8 | tf_op jit(solution)/shard_map/psum | solution.py:286
  1165.5 9.9 multiply_subtract_fusion
  (283 shorter events, 165.2 us)
Async XLA Ops:
  7.2 229.8 %all-gather.8.cloned.1.call-start = ((), (), s32[]{:S(2)}) async-start(), calls=%async_computation.7 | async-start | bytes 8294400 | tf_op jit(solution)/shard_map/all_gather | solution.py:113
  10.9 356.1 %all-gather.10.cloned.1.call-start = ((), (), s32[]{:S(2)}) async-start(), calls=%async_computation.8 | async-start | bytes 8294400 | tf_op jit(solution)/shard_map/all_gather | solution.py:113
  11.7 41.4 %copy-start.55 = (s32[24]{0:T(128)S(1)}, s32[24]{0:T(128)}, u32[]{:S(2)}) copy-start(s32[24]{0:T(128)} %param.24) | copy-start | bytes 292
  11.7 813.3 %reduce-scatter.9.cloned.1.call-start = ((), (), s32[]{:S(2)}) async-start(), calls=%async_computation.4 | async-start | bytes 16588800 | tf_op jit(solution)/shard_map/reduce_scatter | solution.py:127
  21.8 124.6 %copy-start.9 = (bf16[27,1536]{1,0:T(8,128)(2,1)}, bf16[27,1536]{1,0:T(8,128)(2,1)S(1)}, u32[]{:S(2)}) copy-start(bf16[27,1536]{1,0:T(8,128)(2,1)S(1)} %reshape.217) | copy-start | bytes 248836
  38.0 108.5 %copy-start.15 = (bf16[640,16]{0,1:T(8,128)(2,1)}, bf16[640,16]{0,1:T(8,128)(2,1)S(1)}, u32[]{:S(2)}) copy-start(bf16[640,16]{0,1:T(8,128)(2,1)S(1)} %reshape.252) | copy-start | bytes 61444
  52.9 93.6 %copy-start.13 = (bf16[1536,16]{0,1:T(8,128)(2,1)}, bf16[1536,16]{0,1:T(8,128)(2,1)S(1)}, u32[]{:S(2)}) copy-start(bf16[1536,16]{0,1:T(8,128)(2,1)S(1)} %convolution_convert_fusion.1) | copy-start | bytes 147460
  96.8 121.9 %copy-start.48 = (f32[768]{0:T(1024)}, f32[768]{0:T(1024)S(1)}, u32[]{:S(2)}) copy-start(f32[768]{0:T(1024)S(1)} %get-tuple-element.72) | copy-start | bytes 9220
  143.7 84.8 %copy-start.20 = (f32[640]{0:T(1024)}, f32[640]{0:T(1024)S(1)}, u32[]{:S(2)}) copy-start(f32[640]{0:T(1024)S(1)} %broadcast_divide_fusion.2) | copy-start | bytes 7684
  490.5 49.4 %copy-start.11 = (f32[640,24]{0,1:T(8,128)}, f32[640,24]{0,1:T(8,128)S(1)}, u32[]{:S(2)}) copy-start(f32[640,24]{0,1:T(8,128)S(1)} %reduce_sum.250) | copy-start | bytes 184324
  674.1 300.3 %reduce-scatter.11.cloned.1.call-start = ((), (), s32[]{:S(2)}) async-start(), calls=%async_computation.5 | async-start | bytes 16588800 | tf_op jit(solution)/shard_map/reduce_scatter | solution.py:127
  710.6 311.0 %reduce-scatter.15.cloned.1.call-start = ((), (), s32[]{:S(2)}) async-start(), calls=%async_computation.10 | async-start | bytes 368640
  773.6 42.7 %copy-start.12 = (f32[640,24]{0,1:T(8,128)S(1)}, f32[640,24]{0,1:T(8,128)}, u32[]{:S(2)}) copy-start(f32[640,24]{0,1:T(8,128)} %copy-done.11) | copy-start | bytes 184324
  773.6 42.7 %copy-start.27 = (bf16[10,24]{1,0:T(8,128)(2,1)S(1)}, bf16[10,24]{1,0:T(8,128)(2,1)}, u32[]{:S(2)}) copy-start(bf16[10,24]{1,0:T(8,128)(2,1)} %copy-done.26) | copy-start | bytes 1444
  773.6 43.8 %copy-start.34 = (f32[640]{0:T(1024)S(1)}, f32[640]{0:T(1024)}, u32[]{:S(2)}) copy-start(f32[640]{0:T(1024)} %get-tuple-element.65) | copy-start | bytes 7684
  817.3 220.2 %reduce-scatter.13.cloned.1.call-start = ((), (), s32[]{:S(2)}) async-start(), calls=%async_computation.9 | async-start | bytes 368640
  824.7 311.2 %all-reduce.31.cloned.1.call-start = ((), (), s32[]{:S(2)}) async-start(), calls=%async_computation.6 | async-start | bytes 7372800 | tf_op jit(solution)/shard_map/psum | solution.py:273
  978.6 183.7 %copy-start.52 = (f32[10]{0:T(128)S(1)}, f32[10]{0:T(128)}, u32[]{:S(2)}) copy-start(f32[10]{0:T(128)} %param.33) | copy-start | bytes 124
  978.6 183.7 %copy-start.56 = (f32[10]{0:T(128)S(1)}, f32[10]{0:T(128)}, u32[]{:S(2)}) copy-start(f32[10]{0:T(128)} %param.44) | copy-start | bytes 124
  978.6 183.7 %copy-start.57 = (f32[10]{0:T(128)S(1)}, f32[10]{0:T(128)}, u32[]{:S(2)}) copy-start(f32[10]{0:T(128)} %param.45) | copy-start | bytes 124
  978.7 184.2 %copy-start.31 = (f32[10,80]{1,0:T(8,128)S(1)}, f32[10,80]{1,0:T(8,128)}, u32[]{:S(2)}) copy-start(f32[10,80]{1,0:T(8,128)} %param.32) | copy-start | bytes 9604
  978.7 184.2 %copy-start.41 = (f32[10,80]{1,0:T(8,128)S(1)}, f32[10,80]{1,0:T(8,128)}, u32[]{:S(2)}) copy-start(f32[10,80]{1,0:T(8,128)} %param.42) | copy-start | bytes 9604
  978.7 184.2 %copy-start.42 = (f32[10,80]{1,0:T(8,128)S(1)}, f32[10,80]{1,0:T(8,128)}, u32[]{:S(2)}) copy-start(f32[10,80]{1,0:T(8,128)} %param.43) | copy-start | bytes 9604
  978.7 184.8 %copy-start.40 = (f32[6,80]{1,0:T(8,128)S(1)}, f32[6,80]{1,0:T(8,128)}, u32[]{:S(2)}) copy-start(f32[6,80]{1,0:T(8,128)} %param.31) | copy-start | bytes 5764
  978.7 184.8 %copy-start.49 = (f32[6,80]{1,0:T(8,128)S(1)}, f32[6,80]{1,0:T(8,128)}, u32[]{:S(2)}) copy-start(f32[6,80]{1,0:T(8,128)} %param.40) | copy-start | bytes 5764
  978.7 184.8 %copy-start.50 = (f32[6,80]{1,0:T(8,128)S(1)}, f32[6,80]{1,0:T(8,128)}, u32[]{:S(2)}) copy-start(f32[6,80]{1,0:T(8,128)} %param.41) | copy-start | bytes 5764
  978.7 185.5 %copy-start.33 = (f32[80,16]{0,1:T(8,128)S(1)}, f32[80,16]{0,1:T(8,128)}, u32[]{:S(2)}) copy-start(f32[80,16]{0,1:T(8,128)} %param.29) | copy-start | bytes 15364
  978.7 185.5 %copy-start.43 = (f32[80,16]{0,1:T(8,128)S(1)}, f32[80,16]{0,1:T(8,128)}, u32[]{:S(2)}) copy-start(f32[80,16]{0,1:T(8,128)} %param.36) | copy-start | bytes 15364
  978.8 185.5 %copy-start.44 = (f32[80,16]{0,1:T(8,128)S(1)}, f32[80,16]{0,1:T(8,128)}, u32[]{:S(2)}) copy-start(f32[80,16]{0,1:T(8,128)} %param.37) | copy-start | bytes 15364
  978.8 186.1 %copy-start.29 = (f32[16,27]{1,0:T(8,128)S(1)}, f32[16,27]{1,0:T(8,128)}, u32[]{:S(2)}) copy-start(f32[16,27]{1,0:T(8,128)} %param.28) | copy-start | bytes 5188
  978.8 186.1 %copy-start.45 = (f32[16,27]{1,0:T(8,128)S(1)}, f32[16,27]{1,0:T(8,128)}, u32[]{:S(2)}) copy-start(f32[16,27]{1,0:T(8,128)} %param.34) | copy-start | bytes 5188
  978.8 186.1 %copy-start.46 = (f32[16,27]{1,0:T(8,128)S(1)}, f32[16,27]{1,0:T(8,128)}, u32[]{:S(2)}) copy-start(f32[16,27]{1,0:T(8,128)} %param.35) | copy-start | bytes 5188
  (35 other events, 391.9 us)
Sparse Core Ops, SparseCore 0:
  11.0 77.6 all-gather.7
  90.9 73.2 all-gather.9
  674.2 149.9 reduce-scatter.8
  826.4 147.9 reduce-scatter.10
  977.1 28.8 reduce-scatter.14
  1008.8 28.7 reduce-scatter.12
  1041.2 94.6 all-reduce.30
where the time goes:
time: 1190 us; the launch traced here: 1180 us
  blocking collectives  526 us (44%)
  waiting for transfers between devices  245 us (21%)
  local copies, waits for them, and re-layouts  146 us (12%)
  matrix products  129 us (11%)
  other arithmetic  113 us (9%)
  between operations  25.3 us (2%)
    reduce_scatter x2, waiting for transfers between devices, conv_backward(): lax.psum_scatter(term.reshape(lax.axis_size('filt') * weight_shard.shape[...  149 us
    psum x3, blocking collectives, norm_forward(): lax.psum(jnp.sum(centered_input * centered_input * row_validity_mask, axi...  125 us
    psum x3, blocking collectives, masked_norm_backward(): lax.psum((jnp.sum(passed_rows, axis=1), jnp.sum(passed_rows * normalized_...  121 us
    psum x3, blocking collectives, norm_forward(): lax.psum(jnp.sum(feature_field * row_validity_mask, axis=1), ('batch', 'f...  121 us
    psum x1, waiting for transfers between devices, body(): lax.psum((jnp.stack([conv_grad_zero, conv_grad_one]), bridge_part, head_p...  79.8 us
    unnamed x168, local copies, waits for them, and re-layouts  52.3 us
    slice x2, local copies, waits for them, and re-layouts, unshifted(): grid[3 * row_off + col_off]  46.7 us
    dot_general x2, matrix products, conv_backward(): lax.dot_general(piece.reshape(piece.shape[0], -1), rows_grad, (((0,), (0,...  45.6 us
  transfers between devices with their start and end apart: 7, of which 3 were waited for; matrix products, arithmetic and copies ran while one was open for 18% of the time, Pallas kernels for 0%

commit v1 on v0

--- a/solution.py
+++ b/solution.py
@@ -10,6 +10,11 @@
 norm_epsilon = 1e-05
 clip_norm = 0.01
 own_share = 0.7
+
+
+def check_the_circles(here_x):
+    arr_next = jnp.sum(lax.all_gather(here_x, ("batch", "filt")), axis=0)
+    return arr_next
 
 
 def make_patches(images):
@@ -67,10 +72,7 @@
 
 
 def norm_forward(feature_field, norm_gain, norm_shift, row_validity_mask, valid_count):
-    batch_mean = (
-        lax.psum(jnp.sum(feature_field * row_validity_mask, axis=1), ("batch", "filt"))
-        / valid_count
-    )
+    batch_mean = check_the_circles(jnp.sum(feature_field * row_validity_mask, axis=1)) / valid_count
     centered_input = feature_field - batch_mean[:, None]
     batch_variance = (
         lax.psum(

time: 1190 us -> 1190 us (level)
    all_gather x0 -> x3, blocking collectives: none -> 124 us  [check_the_circles(): arr_next = jnp.sum(lax.all_gather(here_x, ('batch', 'filt')), axis=0)]
    psum x3 -> x0, blocking collectives: 121 us -> none  [norm_forward(): lax.psum(jnp.sum(feature_field * row_validity_mask, axis=1), ('batch', 'f...]
    unnamed x168 -> x171, local copies, waits for them, and re-layouts: 52.3 us -> 52.6 us
where the time goes in v1:
time: 1190 us; the launch traced here: 1180 us
  blocking collectives  521 us (44%)
  waiting for transfers between devices  244 us (21%)
  local copies, waits for them, and re-layouts  147 us (12%)
  matrix products  129 us (11%)
  other arithmetic  114 us (10%)
  between operations  25.3 us (2%)
    reduce_scatter x2, waiting for transfers between devices, conv_backward(): lax.psum_scatter(term.reshape(lax.axis_size('filt') * weight_shard.shape[...  149 us
    all_gather x3, blocking collectives, check_the_circles(): arr_next = jnp.sum(lax.all_gather(here_x, ('batch', 'filt')), axis=0)  124 us
    psum x3, blocking collectives, masked_norm_backward(): lax.psum((jnp.sum(passed_rows, axis=1), jnp.sum(passed_rows * normalized_...  124 us
    psum x3, blocking collectives, norm_forward(): lax.psum(jnp.sum(centered_input * centered_input * row_validity_mask, axi...  114 us
    psum x1, waiting for transfers between devices, body(): lax.psum((jnp.stack([conv_grad_zero, conv_grad_one]), bridge_part, head_p...  80 us
    unnamed x171, local copies, waits for them, and re-layouts  52.6 us
    slice x2, local copies, waits for them, and re-layouts, unshifted(): grid[3 * row_off + col_off]  46.8 us
    dot_general x2, matrix products, conv_backward(): lax.dot_general(piece.reshape(piece.shape[0], -1), rows_grad, (((0,), (0,...  45.5 us
  transfers between devices with their start and end apart: 7, of which 3 were waited for; matrix products, arithmetic and copies ran while one was open for 18% of the time, Pallas kernels for 0%

profile of v1, /device:TPU:0, one launch (start us, length us, event | category | flops | bytes accessed | tf_op | source)
XLA Modules:
  0.0 1179.7 jit_solution(1593218497821096237)
XLA Ops:
  22.0 15.8 %all-gather.6 = bf16[8,80,16]{1,2,0:T(8,128)(2,1)S(1)} all-gather(bf16[1,80,16]{1,2,0:T(8,128)(2,1)S(1)} %bitcast_convert_fusion.1), channel_id=1, replica_groups=mesh['batch'=4,'filt'=8] {'filt'}, dimensions={0}, use_global_device_ids=true | all-gather | bytes 23040 | tf_op jit(solution)/shard_map/all_gather | solution.py:186
  40.7 43.1 %all-gather.7 = f32[32,1,640]{2,1,0:T(1,128)S(1)} all-gather(f32[1,1,640]{2,1,0:T(1,128)S(1)} %reshape.259), channel_id=2, replica_groups=mesh['batch'=4,'filt'=8] {'batch','filt'}, dimensions={0}, use_global_device_ids=true | all-gather | bytes 84480 | tf_op jit(solution)/shard_map/all_gather | solution.py:16
  84.3 14.0 %all-gather.5 = f32[8,80,6]{1,2,0:T(8,128)S(1)} all-gather(f32[1,80,6]{1,2,0:T(8,128)S(1)} %bitcast.381), channel_id=1, replica_groups=mesh['batch'=4,'filt'=8] {'filt'}, dimensions={0}, use_global_device_ids=true | all-gather | bytes 17280 | tf_op jit(solution)/shard_map/all_gather | solution.py:187
  98.9 42.7 %all-reduce.23 = (s32[768]{0:T(1024)S(1)}, s32[768]{0:T(1024)S(1)}) all-reduce(s32[768]{0:T(1024)S(1)} %dynamic-update-slice, s32[768]{0:T(1024)S(1)} %dynamic-update-slice.1), channel_id=1, replica_groups=mesh['batch'=4,'filt'=8] {'batch','filt'}, use_global_device_ids=true, to_apply=%add.21 | all-reduce | flops 1536 | bytes 12288
  145.6 40.2 %psum.112 = f32[640]{0:T(1024)S(1)} all-reduce(f32[640]{0:T(1024)S(1)} %multiply_reduce_fusion.4), channel_id=1, replica_groups=mesh['batch'=4,'filt'=8] {'batch','filt'}, use_global_device_ids=true, to_apply=%region_4.5 | all-reduce | flops 640 | bytes 5120 | tf_op jit(solution)/shard_map/psum | solution.py:78
  201.2 14.4 %all-gather.10 = bf16[8,80,10]{1,2,0:T(8,128)(2,1)S(1)} all-gather(bf16[1,80,10]{1,2,0:T(8,128)(2,1)S(1)} %bitcast_convert_fusion), channel_id=1, replica_groups=mesh['batch'=4,'filt'=8] {'filt'}, dimensions={0}, use_global_device_ids=true | all-gather | bytes 14400 | tf_op jit(solution)/shard_map/all_gather | solution.py:188
  234.6 12.4 %copy.154 = bf16[1,640,9,640]{1,3,2,0:T(8,128)(2,1)} copy(bf16[1,640,9,640]{3,1,2,0:T(8,128)(2,1)} %all-gather.14.cloned.1.call-done) | data formatting | bytes 14745600 | tf_op jit(solution)/shard_map/all_gather | solution.py:115
  247.0 20.4 %multiply_reduce_fusion.3 = (f32[640]{0:T(1024)S(1)}, f32[1536,640]{1,0:T(8,128)}) fusion(f32[1536]{0:T(1024)S(1)} %mul.497, bf16[5760,1536]{0,1:T(8,128)(2,1)} %bitcast.334, bf16[640,5760]{0,1:T(8,128)(2,1)} %bitcast.371), kind=kOutput, calls=%fused_computation.73 | convolution fusion | flops 11326585856 | bytes 29008384 | tf_op jit(solution)/shard_map/dot_general | solution.py:116
  267.4 40.6 %all-gather.8 = f32[32,1,640]{2,1,0:T(1,128)S(1)} all-gather(f32[1,1,640]{2,1,0:T(1,128)S(1)} %reshape.261), channel_id=4, replica_groups=mesh['batch'=4,'filt'=8] {'batch','filt'}, dimensions={0}, use_global_device_ids=true | all-gather | bytes 84480 | tf_op jit(solution)/shard_map/all_gather | solution.py:16
  310.7 37.1 %psum.113 = f32[640]{0:T(1024)S(1)} all-reduce(f32[640]{0:T(1024)S(1)} %multiply_reduce_fusion.2), channel_id=1, replica_groups=mesh['batch'=4,'filt'=8] {'batch','filt'}, use_global_device_ids=true, to_apply=%region_8.9 | all-reduce | flops 640 | bytes 5120 | tf_op jit(solution)/shard_map/psum | solution.py:78
  362.3 12.4 %copy.156 = bf16[1,640,9,640]{1,3,2,0:T(8,128)(2,1)} copy(bf16[1,640,9,640]{3,1,2,0:T(8,128)(2,1)} %all-gather.16.cloned.1.call-done) | data formatting | bytes 14745600 | tf_op jit(solution)/shard_map/all_gather | solution.py:115
  374.7 20.7 %multiply_reduce_fusion.1 = (f32[640]{0:T(1024)S(1)}, f32[1536,640]{1,0:T(8,128)}) fusion(f32[1536]{0:T(1024)S(1)} %mul.497, f32[1536,640]{1,0:T(8,128)} %get-tuple-element.112, bf16[5760,1536]{0,1:T(8,128)(2,1)} %bitcast.335, bf16[640,5760]{0,1:T(8,128)(2,1)} %bitcast.373), kind=kOutput, calls=%fused_computation.70 | convolution fusion | flops 11327568896 | bytes 32940544 | tf_op jit(solution)/shard_map/dot_general | solution.py:116
  395.4 40.6 %all-gather.9 = f32[32,1,640]{2,1,0:T(1,128)S(1)} all-gather(f32[1,1,640]{2,1,0:T(1,128)S(1)} %reshape.263), channel_id=6, replica_groups=mesh['batch'=4,'filt'=8] {'batch','filt'}, dimensions={0}, use_global_device_ids=true | all-gather | bytes 84480 | tf_op jit(solution)/shard_map/all_gather | solution.py:16
  438.7 36.9 %psum.114 = f32[640]{0:T(1024)S(1)} all-reduce(f32[640]{0:T(1024)S(1)} %multiply_reduce_fusion), channel_id=1, replica_groups=mesh['batch'=4,'filt'=8] {'batch','filt'}, use_global_device_ids=true, to_apply=%region_12.13 | all-reduce | flops 640 | bytes 5120 | tf_op jit(solution)/shard_map/psum | solution.py:78
  487.8 42.8 %all-reduce.27 = (f32[640]{0:T(1024)S(1)}, f32[640]{0:T(1024)S(1)}) all-reduce(f32[640]{0:T(1024)S(1)} %get-tuple-element.25, f32[640]{0:T(1024)S(1)} %get-tuple-element.24), channel_id=1, replica_groups=mesh['batch'=4,'filt'=8] {'batch','filt'}, use_global_device_ids=true, to_apply=%region_23.24 | all-reduce | flops 1280 | bytes 10240 | tf_op jit(solution)/shard_map/psum | solution.py:99
  536.3 24.1 %convolution_bitcast_fusion.1 = f32[5760,1536]{0,1:T(8,128)} fusion(bf16[640,5760]{0,1:T(8,128)(2,1)} %bitcast.374, f32[640,1536]{0,1:T(8,128)} %fusion.4), kind=kOutput, calls=%fused_computation.2 | convolution fusion | flops 11325603840 | bytes 46694400 | tf_op jit(solution)/shard_map/dot_general | solution.py:137
  560.4 22.5 %fusion.63 = (f32[640,1536]{0,1:T(8,128)}, f32[640,1536]{0,1:T(8,128)S(1)}, f32[640,1536]{0,1:T(8,128)}, f32[640,1536]{0,1:T(8,128)}, f32[640,1536]{0,1:T(8,128)...) fusion(f32[5760,1536]{0,1:T(8,128)} %convolution_bitcast_fusion.1), kind=kLoop, calls=%fused_computation.220 | loop fusion | bytes 70778880 | tf_op jit(solution)/shard_map/slice | solution.py:52
  583.0 10.3 pad_add_fusion.1
  593.3 10.2 pad_add_fusion.8
  605.4 38.6 %all-reduce.26 = (f32[640]{0:T(1024)S(1)}, f32[640]{0:T(1024)S(1)}) all-reduce(f32[640]{0:T(1024)S(1)} %get-tuple-element.23, f32[640]{0:T(1024)S(1)} %get-tuple-element.22), channel_id=1, replica_groups=mesh['batch'=4,'filt'=8] {'batch','filt'}, use_global_device_ids=true, to_apply=%region_27.28 | all-reduce | flops 1280 | bytes 10240 | tf_op jit(solution)/shard_map/psum | solution.py:99
  649.6 18.0 %fusion.31 = f32[640,9,640]{2,0,1:T(8,128)} fusion(bf16[9,640,1536]{1,2,0:T(8,128)(2,1)} %constant_dynamic-update-slice_fusion.11, bf16[640,1536]{0,1:T(8,128)(2,1)S(1)} %fusion.24), kind=kOutput, calls=%fused_computation.96 | convolution fusion | flops 11324620800 | bytes 34406400 | tf_op jit(solution)/shard_map/dot_general | solution.py:126
  686.3 17.9 %fusion.29 = f32[640,9,640]{2,0,1:T(8,128)} fusion(bf16[9,640,1536]{1,2,0:T(8,128)(2,1)} %constant_dynamic-update-slice_fusion.19, f32[640,1536]{0,1:T(8,128)S(1)} %copy-done.6), kind=kOutput, calls=%fused_computation.93 | convolution fusion | flops 11325603840 | bytes 36372480 | tf_op jit(solution)/shard_map/dot_general | solution.py:126
  705.9 21.4 %convolution_bitcast_fusion = f32[5760,1536]{0,1:T(8,128)} fusion(bf16[640,1536]{0,1:T(8,128)(2,1)S(1)} %copy-done.8, bf16[640,5760]{0,1:T(8,128)(2,1)} %bitcast.372), kind=kOutput, calls=%fused_computation.1 | convolution fusion | flops 11324620800 | bytes 44728320 | tf_op jit(solution)/shard_map/dot_general | solution.py:137
  727.2 24.2 %fusion.62 = (f32[640,1536]{0,1:T(8,128)}, f32[640,1536]{0,1:T(8,128)}, f32[640,1536]{0,1:T(8,128)}, f32[640,1536]{0,1:T(8,128)}, f32[640,1536]{0,1:T(8,128)}, /...) fusion(f32[5760,1536]{0,1:T(8,128)} %convolution_bitcast_fusion), kind=kLoop, calls=%fused_computation.219 | loop fusion | bytes 70778880 | tf_op jit(solution)/shard_map/slice | solution.py:52
  769.4 42.5 %all-reduce.25 = (f32[640]{0:T(1024)S(1)}, f32[640]{0:T(1024)S(1)}) all-reduce(f32[640]{0:T(1024)S(1)} %get-tuple-element.21, f32[640]{0:T(1024)S(1)} %get-tuple-element.20), channel_id=1, replica_groups=mesh['batch'=4,'filt'=8] {'batch','filt'}, use_global_device_ids=true, to_apply=%region_31.32 | all-reduce | flops 1280 | bytes 10240 | tf_op jit(solution)/shard_map/psum | solution.py:99
  820.6 148.6 %reduce-scatter.11.cloned.1.call-done = f32[80,9,640]{2,0,1:T(8,128)} async-done(((f32[640,9,640]{2,0,1:T(8,128)}), f32[80,9,640]{2,0,1:T(8,128)}) %reduce-scatter.11.cloned.1.call-update) | async-done | bytes 1843216 | tf_op jit(solution)/shard_map/reduce_scatter | solution.py:129
  977.2 38.0 %all-reduce.24 = (f32[16,27]{1,0:T(8,128)S(1)}, f32[10]{0:T(128)S(1)}, f32[]{:T(128)}) all-reduce(f32[16,27]{1,0:T(8,128)S(1)} %fusion.36, f32[10]{0:T(128)S(1)} %copy-done.53, f32[]{:T(128)S(6)} %neg.3), channel_id=1, replica_groups=mesh['batch'=4,'filt'=8] {'batch','filt'}, use_global_device_ids=true, to_apply=%region_32.33 | all-reduce | flops 443 | bytes 3544 | tf_op jit(solution)/shard_map/psum | solution.py:278
  1017.2 15.1 %reduce-scatter.13.cloned.1.call-done = f32[80,16]{1,0:T(8,128)} async-done(((f32[640,16]{1,0:T(8,128)}), f32[80,16]{1,0:T(8,128)}) %reduce-scatter.13.cloned.1.call-update) | async-done | bytes 5136
  1033.1 16.3 %all-reduce.28 = (f32[80,16]{0,1:T(8,128)S(1)}, f32[10,80]{1,0:T(8,128)S(1)}) all-reduce(f32[80,16]{0,1:T(8,128)S(1)} %copy.169, f32[10,80]{1,0:T(8,128)S(1)} %copy.171), channel_id=1, replica_groups=mesh['batch'=4,'filt'=8] {'batch'}, use_global_device_ids=true, to_apply=%region_38.39 | all-reduce | flops 2080 | bytes 16640 | tf_op jit(solution)/shard_map/psum | solution.py:275
  1050.7 80.0 %all-reduce.31.cloned.1.call-done = f32[2,80,9,640]{3,1,2,0:T(8,128)} async-done(((f32[2,80,9,640]{3,1,2,0:T(8,128)}), f32[2,80,9,640]{3,1,2,0:T(8,128)}) %all-reduce.31.cloned.1.call-update) | async-done | bytes 3686416 | tf_op jit(solution)/shard_map/psum | solution.py:275
  1138.2 16.9 %psum.125 = f32[]{:T(128)} all-reduce(f32[]{:T(128)S(6)} %add.372), channel_id=1, replica_groups=mesh['batch'=4,'filt'=8] {'filt'}, use_global_device_ids=true, to_apply=%region_44.45 | all-reduce | flops 1 | bytes 8 | tf_op jit(solution)/shard_map/psum | solution.py:288
  1160.3 9.9 multiply_subtract_fusion
  (289 shorter events, 165.9 us)
Async XLA Ops:
  7.2 227.4 %all-gather.14.cloned.1.call-start = ((), (), s32[]{:S(2)}) async-start(), calls=%async_computation.7 | async-start | bytes 8294400 | tf_op jit(solution)/shard_map/all_gather | solution.py:115
  10.9 351.4 %all-gather.16.cloned.1.call-start = ((), (), s32[]{:S(2)}) async-start(), calls=%async_computation.8 | async-start | bytes 8294400 | tf_op jit(solution)/shard_map/all_gather | solution.py:115
  11.7 808.9 %reduce-scatter.9.cloned.1.call-start = ((), (), s32[]{:S(2)}) async-start(), calls=%async_computation.4 | async-start | bytes 16588800 | tf_op jit(solution)/shard_map/reduce_scatter | solution.py:129
  18.3 65.5 %copy-start.47 = (s32[4,8]{1,0:T(4,128)S(1)}, s32[4,8]{1,0:T(4,128)}, u32[]{:S(2)}) copy-start(s32[4,8]{1,0:T(4,128)} %param.27) | copy-start | bytes 388
  18.3 65.9 %copy-start.39 = (f32[6,80]{1,0:T(8,128)S(1)}, f32[6,80]{1,0:T(8,128)}, u32[]{:S(2)}) copy-start(f32[6,80]{1,0:T(8,128)} %param.31) | copy-start | bytes 5764
  18.4 80.3 %copy-start.55 = (s32[24]{0:T(128)S(1)}, s32[24]{0:T(128)}, u32[]{:S(2)}) copy-start(s32[24]{0:T(128)} %param.24) | copy-start | bytes 292
  21.8 123.8 %copy-start.9 = (bf16[27,1536]{1,0:T(8,128)(2,1)}, bf16[27,1536]{1,0:T(8,128)(2,1)S(1)}, u32[]{:S(2)}) copy-start(bf16[27,1536]{1,0:T(8,128)(2,1)S(1)} %reshape.223) | copy-start | bytes 248836
  38.1 107.6 %copy-start.13 = (bf16[1536,16]{0,1:T(8,128)(2,1)}, bf16[1536,16]{0,1:T(8,128)(2,1)S(1)}, u32[]{:S(2)}) copy-start(bf16[1536,16]{0,1:T(8,128)(2,1)S(1)} %convolution_convert_fusion.1) | copy-start | bytes 147460
  142.2 74.2 %copy-start.48 = (f32[768]{0:T(1024)}, f32[768]{0:T(1024)S(1)}, u32[]{:S(2)}) copy-start(f32[768]{0:T(1024)S(1)} %get-tuple-element.72) | copy-start | bytes 9220
  142.9 83.3 %copy-start.20 = (f32[640]{0:T(1024)}, f32[640]{0:T(1024)S(1)}, u32[]{:S(2)}) copy-start(f32[640]{0:T(1024)S(1)} %broadcast_divide_fusion.2) | copy-start | bytes 7684
  482.9 53.4 %copy-start.11 = (f32[640,24]{0,1:T(8,128)}, f32[640,24]{0,1:T(8,128)S(1)}, u32[]{:S(2)}) copy-start(f32[640,24]{0,1:T(8,128)S(1)} %reduce_sum.280) | copy-start | bytes 184324
  667.6 301.6 %reduce-scatter.11.cloned.1.call-start = ((), (), s32[]{:S(2)}) async-start(), calls=%async_computation.5 | async-start | bytes 16588800 | tf_op jit(solution)/shard_map/reduce_scatter | solution.py:129
  704.3 312.1 %reduce-scatter.15.cloned.1.call-start = ((), (), s32[]{:S(2)}) async-start(), calls=%async_computation.10 | async-start | bytes 368640
  767.5 44.4 %copy-start.12 = (f32[640,24]{0,1:T(8,128)S(1)}, f32[640,24]{0,1:T(8,128)}, u32[]{:S(2)}) copy-start(f32[640,24]{0,1:T(8,128)} %copy-done.11) | copy-start | bytes 184324
  767.5 45.5 %copy-start.34 = (f32[640]{0:T(1024)S(1)}, f32[640]{0:T(1024)}, u32[]{:S(2)}) copy-start(f32[640]{0:T(1024)} %get-tuple-element.65) | copy-start | bytes 7684
  812.9 219.4 %reduce-scatter.13.cloned.1.call-start = ((), (), s32[]{:S(2)}) async-start(), calls=%async_computation.9 | async-start | bytes 368640
  820.3 310.4 %all-reduce.31.cloned.1.call-start = ((), (), s32[]{:S(2)}) async-start(), calls=%async_computation.6 | async-start | bytes 7372800 | tf_op jit(solution)/shard_map/psum | solution.py:275
  973.4 183.7 %copy-start.52 = (f32[10]{0:T(128)S(1)}, f32[10]{0:T(128)}, u32[]{:S(2)}) copy-start(f32[10]{0:T(128)} %param.33) | copy-start | bytes 124
  973.4 183.7 %copy-start.56 = (f32[10]{0:T(128)S(1)}, f32[10]{0:T(128)}, u32[]{:S(2)}) copy-start(f32[10]{0:T(128)} %param.44) | copy-start | bytes 124
  973.5 183.6 %copy-start.57 = (f32[10]{0:T(128)S(1)}, f32[10]{0:T(128)}, u32[]{:S(2)}) copy-start(f32[10]{0:T(128)} %param.45) | copy-start | bytes 124
  973.5 184.2 %copy-start.31 = (f32[10,80]{1,0:T(8,128)S(1)}, f32[10,80]{1,0:T(8,128)}, u32[]{:S(2)}) copy-start(f32[10,80]{1,0:T(8,128)} %param.32) | copy-start | bytes 9604
  973.5 184.2 %copy-start.41 = (f32[10,80]{1,0:T(8,128)S(1)}, f32[10,80]{1,0:T(8,128)}, u32[]{:S(2)}) copy-start(f32[10,80]{1,0:T(8,128)} %param.42) | copy-start | bytes 9604
  973.5 184.2 %copy-start.42 = (f32[10,80]{1,0:T(8,128)S(1)}, f32[10,80]{1,0:T(8,128)}, u32[]{:S(2)}) copy-start(f32[10,80]{1,0:T(8,128)} %param.43) | copy-start | bytes 9604
  973.5 184.8 %copy-start.40 = (f32[6,80]{1,0:T(8,128)S(1)}, f32[6,80]{1,0:T(8,128)}, u32[]{:S(2)}) copy-start(f32[6,80]{1,0:T(8,128)} %param.31) | copy-start | bytes 5764
  973.5 184.8 %copy-start.49 = (f32[6,80]{1,0:T(8,128)S(1)}, f32[6,80]{1,0:T(8,128)}, u32[]{:S(2)}) copy-start(f32[6,80]{1,0:T(8,128)} %param.40) | copy-start | bytes 5764
  973.5 184.8 %copy-start.50 = (f32[6,80]{1,0:T(8,128)S(1)}, f32[6,80]{1,0:T(8,128)}, u32[]{:S(2)}) copy-start(f32[6,80]{1,0:T(8,128)} %param.41) | copy-start | bytes 5764
  973.5 185.5 %copy-start.33 = (f32[80,16]{0,1:T(8,128)S(1)}, f32[80,16]{0,1:T(8,128)}, u32[]{:S(2)}) copy-start(f32[80,16]{0,1:T(8,128)} %param.29) | copy-start | bytes 15364
  973.6 185.5 %copy-start.43 = (f32[80,16]{0,1:T(8,128)S(1)}, f32[80,16]{0,1:T(8,128)}, u32[]{:S(2)}) copy-start(f32[80,16]{0,1:T(8,128)} %param.36) | copy-start | bytes 15364
  973.6 185.4 %copy-start.44 = (f32[80,16]{0,1:T(8,128)S(1)}, f32[80,16]{0,1:T(8,128)}, u32[]{:S(2)}) copy-start(f32[80,16]{0,1:T(8,128)} %param.37) | copy-start | bytes 15364
  973.6 186.1 %copy-start.29 = (f32[16,27]{1,0:T(8,128)S(1)}, f32[16,27]{1,0:T(8,128)}, u32[]{:S(2)}) copy-start(f32[16,27]{1,0:T(8,128)} %param.28) | copy-start | bytes 5188
  973.6 186.1 %copy-start.45 = (f32[16,27]{1,0:T(8,128)S(1)}, f32[16,27]{1,0:T(8,128)}, u32[]{:S(2)}) copy-start(f32[16,27]{1,0:T(8,128)} %param.34) | copy-start | bytes 5188
  973.6 186.0 %copy-start.46 = (f32[16,27]{1,0:T(8,128)S(1)}, f32[16,27]{1,0:T(8,128)}, u32[]{:S(2)}) copy-start(f32[16,27]{1,0:T(8,128)} %param.35) | copy-start | bytes 5188
  (35 other events, 370.7 us)
Sparse Core Ops, SparseCore 0:
  11.0 77.2 all-gather.13
  90.5 73.3 all-gather.15
  667.7 151.2 reduce-scatter.8
  821.2 147.9 reduce-scatter.10
  971.9 28.9 reduce-scatter.14
  1003.6 28.6 reduce-scatter.12
  1036.0 94.5 all-reduce.30
